TPU v7x, 128 devices: a whole 4x4x4 slice. The times are simulated.
128 devices in a mesh: dp: 2 (over core), expert: 64 (over x, y, z).
Axes of the slice: x: 4, y: 4, z: 4, core: 2. Of those that a mesh axis runs over, the one named last changes fastest.
Arguments:
- tokens: bfloat16 [64, 512, 1024], P('expert', 'dp'), may hold values from -6 to 6
- teacher: bfloat16 [64, 512, 1024], P('expert', 'dp'), may hold values from -6 to 6
- lengths: int32 [64], P('expert'), may hold values from 128 to 512, as said below
- routes: int32 [64, 512, 1], P('expert', 'dp'), may hold values from 0 to 63; in each aligned block of 256 rows (0 to 255, 256 to 511, ..., all dimensions but the last counted through in order) at most 8 rows name the same one
- ln1_gain: bfloat16 [1024], P(('dp', 'expert')), may hold values from 0.5 to 1.5
- ln1_bias: bfloat16 [1024], P(('dp', 'expert')), may hold values from -1.75 to 1.75
- query_key_value_weight: bfloat16 [1024, 3072], P(('dp', 'expert')), may hold values from -0.1875 to 0.1875
- output_weight: bfloat16 [1024, 1024], P(('dp', 'expert')), may hold values from -1.5 to 1.5
- ln2_gain: bfloat16 [1024], P(('dp', 'expert')), may hold values from 0.5 to 1.5
- ln2_bias: bfloat16 [1024], P(('dp', 'expert')), may hold values from -1.75 to 1.75
- router_weight: bfloat16 [1024, 64], P(('dp', 'expert')), may hold values from -0.125 to 0.125
- w_in: bfloat16 [64, 1024, 4096], P('expert', 'dp'), may hold values from -0.1875 to 0.1875
- w_down: bfloat16 [64, 4096, 1024], P('expert', 'dp'), may hold values from -6 to 6
Outputs:
- mixed_out: bfloat16 [64, 512, 1024], P('expert', 'dp')
- loss_value: float32 [], replicated
- grad_tokens: float32 [64, 512, 1024], P('expert', 'dp')
- grad_ln1_gain: float32 [1024], P(('dp', 'expert'))
- grad_ln1_bias: float32 [1024], P(('dp', 'expert'))
- grad_w_qkv: float32 [1024, 3072], P(('dp', 'expert'))
- grad_w_out: float32 [1024, 1024], P(('dp', 'expert'))
- grad_ln2_gain: float32 [1024], P(('dp', 'expert'))
- grad_ln2_bias: float32 [1024], P(('dp', 'expert'))
- grad_w_router: float32 [1024, 64], P(('dp', 'expert'))
- grad_w_in: float32 [64, 1024, 4096], P('expert', 'dp')
- grad_w_down: float32 [64, 4096, 1024], P('expert', 'dp')
Inputs may be any that keep to these rules, and one draw needn't show every extreme that they name: `lengths`: some slot has exactly 512 valid tokens in every draw; the tokens of a slot past its length are padding. `routes`: within the rows of one device (aligned blocks of 256 positions of a slot) no expert is named more than 8 times, and 8 is reached.
All inputs are finite; a program needn't handle non-finite values.
Results may differ from a plain program's by a relative error of at most 0.012.
Values may be sent and summed in bfloat16 or wider, within the bound.
A program may use at most 192 MiB of HBM per device.

v0:
```python
import jax
import jax.numpy as jnp
from jax import lax
from jax.sharding import PartitionSpec as P

HEADS = 16


def layer_norm(values, scale_vec, offset):
    center = jnp.mean(values, -1, keepdims=True)
    centred = values - center
    spread = jnp.mean(centred * centred, -1, keepdims=True)
    inverse = lax.rsqrt(spread + 1e-05)
    normed = centred * inverse
    return (normed * scale_vec + offset, normed, inverse)


def norm_back(upstream, normed, inverse, scale_vec):
    scaled = upstream * scale_vec
    average = jnp.mean(scaled, -1, keepdims=True)
    project = jnp.mean(scaled * normed, -1, keepdims=True)
    return (
        inverse * (scaled - average - normed * project),
        jnp.sum(upstream * normed, 0),
        jnp.sum(upstream, 0),
    )


def times_transposed(left_mat, right_mat):
    return lax.dot_general(
        left_mat, right_mat, (((1,), (1,)), ((), ())), preferred_element_type=jnp.float32
    )


def transposed_times(left_mat, right_mat):
    return lax.dot_general(
        left_mat, right_mat, (((0,), (0,)), ((), ())), preferred_element_type=jnp.float32
    )


def per_device(
    tokens,
    teacher,
    lengths,
    routes,
    ln1_gain,
    ln1_bias,
    query_key_value_weight,
    output_weight,
    ln2_gain,
    ln2_bias,
    router_weight,
    w_in,
    w_down,
):
    group = tokens.shape[1]
    width = tokens.shape[2]
    head_dim = width // HEADS
    sources = lax.axis_size("expert")
    seq_len = group * lax.axis_size("dp")
    capacity = max(2, 2 * group // sources)
    layer_shards = (
        ln1_gain,
        ln1_bias,
        query_key_value_weight,
        output_weight,
        ln2_gain,
        ln2_bias,
        router_weight,
    )
    gathered = (
        lax.all_gather(layer_shards[0], ("dp", "expert"), axis=0, tiled=True),
        lax.all_gather(layer_shards[1], ("dp", "expert"), axis=0, tiled=True),
        lax.all_gather(layer_shards[2], ("dp", "expert"), axis=0, tiled=True),
        lax.all_gather(layer_shards[3], ("dp", "expert"), axis=0, tiled=True),
        lax.all_gather(layer_shards[4], ("dp", "expert"), axis=0, tiled=True),
        lax.all_gather(layer_shards[5], ("dp", "expert"), axis=0, tiled=True),
        lax.all_gather(layer_shards[6], ("dp", "expert"), axis=0, tiled=True),
    )
    experts_whole = (
        lax.all_gather(w_in, "dp", axis=1, tiled=True),
        lax.all_gather(w_down, "dp", axis=1, tiled=True),
    )
    w_first = experts_whole[0][0]
    w_second = experts_whole[1][0]
    gain_one = gathered[0].astype(jnp.float32)
    bias_one = gathered[1].astype(jnp.float32)
    gain_two = gathered[4].astype(jnp.float32)
    bias_two = gathered[5].astype(jnp.float32)
    inputs = tokens[0].astype(jnp.float32)
    norm_full, normed_one, inverse_one = layer_norm(inputs, gain_one, bias_one)
    first_norm = norm_full.astype(jnp.bfloat16)
    query_key_value_rows = jnp.dot(
        first_norm, gathered[2], preferred_element_type=jnp.float32
    ).astype(jnp.bfloat16)
    queries = query_key_value_rows[:, :width].reshape(group, HEADS, head_dim)
    kv_whole = lax.all_gather(query_key_value_rows[:, width:], "dp", axis=0, tiled=True)
    key_rows = kv_whole[:, :width].reshape(seq_len, HEADS, head_dim)
    value_rows = kv_whole[:, width:].reshape(seq_len, HEADS, head_dim)
    query_pos = lax.axis_index("dp") * group + jnp.arange(group)
    key_pos = jnp.arange(seq_len)
    allowed = (key_pos[None, :] <= query_pos[:, None]) & (key_pos[None, :] < lengths[0])

    def score_block():
        scaled_raw = (
            jnp.einsum("qhd,khd->hqk", queries, key_rows, preferred_element_type=jnp.float32)
            * 0.125
        )
        return jnp.where(allowed[None], scaled_raw, -1e30)

    scores = score_block()
    maximum = jnp.max(scores, -1, keepdims=True)
    exponent = jnp.exp(scores - maximum)
    denominator = jnp.sum(exponent, -1, keepdims=True)
    log_total = maximum + jnp.log(denominator)
    probs_low = (exponent / denominator).astype(jnp.bfloat16)
    attention_result = jnp.einsum(
        "hqk,khd->qhd", probs_low, value_rows, preferred_element_type=jnp.float32
    )
    attention_result = attention_result.reshape(group, width).astype(jnp.bfloat16)
    residual_branch = jnp.dot(attention_result, gathered[3], preferred_element_type=jnp.float32)
    residual = inputs + residual_branch
    norm_two_full, normed_two, inverse_two = layer_norm(residual, gain_two, bias_two)
    second_norm = norm_two_full.astype(jnp.bfloat16)
    router_scores = jnp.dot(second_norm, gathered[6], preferred_element_type=jnp.float32)
    router_probs = jax.nn.softmax(router_scores, -1)
    route_ids = routes[0, :, 0]
    chosen = route_ids[:, None] == jnp.arange(sources)[None, :]
    gate_prob = jnp.sum(jnp.where(chosen, router_probs, 0.0), -1)
    ranking = jnp.cumsum(chosen.astype(jnp.int32), 0) - 1
    slot_ids = route_ids * capacity + jnp.sum(jnp.where(chosen, ranking, 0), -1)
    placing = (jnp.arange(sources * capacity)[:, None] == slot_ids[None, :]).astype(jnp.bfloat16)
    outgoing = jnp.dot(placing, second_norm, preferred_element_type=jnp.float32).astype(
        jnp.bfloat16
    )
    outgoing = outgoing.reshape(sources, capacity, width)
    received = lax.all_to_all(outgoing, "expert", split_axis=0, concat_axis=0, tiled=True)
    per_source = received.shape[1]
    flat_rows = received.reshape(-1, width)
    pre_act = jnp.dot(flat_rows, w_first, preferred_element_type=jnp.float32)
    activated = jax.nn.gelu(pre_act, approximate=True).astype(jnp.bfloat16)
    result_rows = jnp.dot(activated, w_second, preferred_element_type=jnp.float32).astype(
        jnp.bfloat16
    )
    produced = result_rows.reshape(sources, per_source, width)
    pre_kept = pre_act.reshape(sources, per_source, -1)
    returned = lax.all_to_all(produced, "expert", split_axis=0, concat_axis=0, tiled=True)
    expert_out = transposed_times(placing, returned.reshape(-1, width))
    mixed_out = (residual + gate_prob[:, None] * expert_out).astype(jnp.bfloat16)
    valid_rows = (query_pos < lengths[0]).astype(jnp.float32)
    errors = mixed_out.astype(jnp.float32) - teacher[0].astype(jnp.float32)
    totals = lax.psum(
        (jnp.sum(valid_rows[:, None] * errors * errors), jnp.sum(valid_rows)), ("dp", "expert")
    )
    loss_value = totals[0] / (totals[1] * width)
    layer_back = (
        lax.all_gather(layer_shards[0], ("dp", "expert"), axis=0, tiled=True),
        lax.all_gather(layer_shards[1], ("dp", "expert"), axis=0, tiled=True),
        lax.all_gather(layer_shards[2], ("dp", "expert"), axis=0, tiled=True),
        lax.all_gather(layer_shards[3], ("dp", "expert"), axis=0, tiled=True),
        lax.all_gather(layer_shards[4], ("dp", "expert"), axis=0, tiled=True),
        lax.all_gather(layer_shards[5], ("dp", "expert"), axis=0, tiled=True),
        lax.all_gather(layer_shards[6], ("dp", "expert"), axis=0, tiled=True),
    )
    experts_back = (
        lax.all_gather(w_in, "dp", axis=1, tiled=True),
        lax.all_gather(w_down, "dp", axis=1, tiled=True),
    )
    first_back = experts_back[0][0]
    second_back = experts_back[1][0]
    d_mixed = valid_rows[:, None] * errors
    d_gate = jnp.sum(d_mixed * expert_out, -1)
    d_expert = (gate_prob[:, None] * d_mixed).astype(jnp.bfloat16)
    d_send = jnp.dot(placing, d_expert, preferred_element_type=jnp.float32).astype(jnp.bfloat16)
    d_recv = lax.all_to_all(
        d_send.reshape(sources, capacity, width), "expert", split_axis=0, concat_axis=0, tiled=True
    ).reshape(-1, width)
    pre_rows = pre_kept.reshape(d_recv.shape[0], -1)
    d_act = times_transposed(d_recv, second_back)
    act_rows, gelu_back = jax.vjp(lambda inner: jax.nn.gelu(inner, approximate=True), pre_rows)
    d_pre = gelu_back(d_act)[0].astype(jnp.bfloat16)
    act_low = act_rows.astype(jnp.bfloat16)
    arrived_rows = received.reshape(-1, width)
    d_rows = (
        times_transposed(d_pre, first_back).astype(jnp.bfloat16).reshape(sources, capacity, width)
    )
    d_back = lax.all_to_all(d_rows, "expert", split_axis=0, concat_axis=0, tiled=True)
    d_norm_expert = transposed_times(placing, d_back.reshape(-1, width))
    d_logits = (d_gate * gate_prob)[:, None] * (chosen.astype(jnp.float32) - router_probs)
    router_full = layer_back[6].astype(jnp.float32)
    grad_router = jnp.dot(
        second_norm.astype(jnp.float32).T, d_logits, precision=lax.Precision.HIGHEST
    )
    d_norm_two = d_norm_expert + jnp.dot(d_logits, router_full.T, precision=lax.Precision.HIGHEST)
    d_resid_part, grad_gain_two, grad_bias_two = norm_back(
        d_norm_two, normed_two, inverse_two, gain_two
    )
    d_resid = d_mixed + d_resid_part
    d_branch = d_resid.astype(jnp.bfloat16)
    grad_out = transposed_times(attention_result, d_branch)
    d_attended = (
        times_transposed(d_branch, layer_back[3])
        .astype(jnp.bfloat16)
        .reshape(group, HEADS, head_dim)
    )
    probs_again = jnp.exp(score_block() - log_total)
    d_probs = jnp.einsum("qhd,khd->hqk", d_attended, value_rows, preferred_element_type=jnp.float32)
    delta_sum = jnp.sum(probs_again * d_probs, -1, keepdims=True)
    d_scores = (probs_again * (d_probs - delta_sum)).astype(jnp.bfloat16)
    d_queries = (
        jnp.einsum("hqk,khd->qhd", d_scores, key_rows, preferred_element_type=jnp.float32) * 0.125
    )
    d_keys = (
        jnp.einsum("hqk,qhd->khd", d_scores, queries, preferred_element_type=jnp.float32) * 0.125
    )
    d_values = jnp.einsum("hqk,qhd->khd", probs_low, d_attended, preferred_element_type=jnp.float32)
    d_kv_whole = jnp.concatenate(
        [d_keys.reshape(seq_len, width), d_values.reshape(seq_len, width)], 1
    )
    d_kv = lax.psum_scatter(d_kv_whole.astype(jnp.bfloat16), "dp", scatter_dimension=0, tiled=True)
    d_qkv = jnp.concatenate([d_queries.reshape(group, width).astype(jnp.bfloat16), d_kv], 1)
    grad_qkv = transposed_times(first_norm, d_qkv)
    d_norm_one = times_transposed(d_qkv, layer_back[2])
    d_input_part, grad_gain_one, grad_bias_one = norm_back(
        d_norm_one, normed_one, inverse_one, gain_one
    )
    grad_tokens = d_resid + d_input_part
    layer_grads = (
        lax.psum_scatter(grad_gain_one, ("dp", "expert"), scatter_dimension=0, tiled=True),
        lax.psum_scatter(grad_bias_one, ("dp", "expert"), scatter_dimension=0, tiled=True),
        lax.psum_scatter(grad_qkv, ("dp", "expert"), scatter_dimension=0, tiled=True),
        lax.psum_scatter(grad_out, ("dp", "expert"), scatter_dimension=0, tiled=True),
        lax.psum_scatter(grad_gain_two, ("dp", "expert"), scatter_dimension=0, tiled=True),
        lax.psum_scatter(grad_bias_two, ("dp", "expert"), scatter_dimension=0, tiled=True),
        lax.psum_scatter(grad_router, ("dp", "expert"), scatter_dimension=0, tiled=True),
    )
    grad_down = transposed_times(act_low, d_recv)
    grad_in = transposed_times(arrived_rows, d_pre)
    expert_grads = (
        lax.psum_scatter(
            grad_in[None].astype(jnp.bfloat16), "dp", scatter_dimension=1, tiled=True
        ).astype(jnp.float32),
        lax.psum_scatter(
            grad_down[None].astype(jnp.bfloat16), "dp", scatter_dimension=1, tiled=True
        ).astype(jnp.float32),
    )
    grad_in_out = expert_grads[0]
    grad_down_out = expert_grads[1]
    return (
        mixed_out[None],
        loss_value,
        grad_tokens[None],
        layer_grads[0],
        layer_grads[1],
        layer_grads[2],
        layer_grads[3],
        layer_grads[4],
        layer_grads[5],
        layer_grads[6],
        grad_in_out,
        grad_down_out,
    )


def solution(mesh):
    placed = (
        P("expert", "dp", None),
        P("expert", "dp", None),
        P("expert"),
        P("expert", "dp", None),
        P(("dp", "expert")),
        P(("dp", "expert")),
        P(("dp", "expert"), None),
        P(("dp", "expert"), None),
        P(("dp", "expert")),
        P(("dp", "expert")),
        P(("dp", "expert"), None),
        P("expert", "dp", None),
        P("expert", "dp", None),
    )
    return jax.shard_map(
        per_device,
        mesh=mesh,
        in_specs=placed,
        out_specs=(
            P("expert", "dp", None),
            P(),
            P("expert", "dp", None),
            P(("dp", "expert")),
            P(("dp", "expert")),
            P(("dp", "expert"), None),
            P(("dp", "expert"), None),
            P(("dp", "expert")),
            P(("dp", "expert")),
            P(("dp", "expert"), None),
            P("expert", "dp", None),
            P("expert", "dp", None),
        ),
        check_vma=False,
    )
```

profile of v0, /device:TPU:0, one launch (start us, length us, event | category | flops | bytes accessed | tf_op | source)
XLA Modules:
  0.0 1750.9 jit_solution(15812579265800073701)
XLA Ops:
  11.3 69.1 %all-reduce.10 = (bf16[1024]{0:T(1024)(128)(2,1)S(1)}, bf16[1024]{0:T(1024)(128)(2,1)S(1)}, bf16[1024]{0:T(1024)(128)(2,1)S(1)}, bf16[1024]{0:T(1024)(128)(2,1)S(1)}) all-reduce(bf16[1024]{0:T(1024)(128)(2,1)S(1)} %dynamic-update-slice.1, bf16[1024]{0:T(1024)(128)(2,1)S(1)} %dynamic-update-slice, ...), channel_id=1, replica_groups=mesh['dp'=2,'expert'=64] {'dp','expert'}, use_global_device_ids=true, to_apply=%add.1 | all-reduce | flops 4096 | bytes 16384
  83.1 4.9 convolution_convert_fusion
  93.1 6.1 all-gather.8.cloned.1.call-done
  99.2 2.7 fusion.94
  113.9 54.9 %all-gather.10.cloned.1.call-done = bf16[1024,1024]{1,0:T(8,128)(2,1)} async-done(((bf16[8,1024]{1,0:T(8,128)(2,1)}), bf16[1024,1024]{1,0:T(8,128)(2,1)}) %all-gather.10.cloned.1.call-update) | async-done | bytes 2097168 | tf_op jit(solution)/shard_map/all_gather | solution.py:75
  173.2 6.5 all-to-all-start
  179.7 10.6 all-gather.12.cloned.1.call-done
  190.3 8.4 all-to-all-done
  199.7 10.9 fusion.13
  210.7 5.1 all-gather.14.cloned.1.call-done
  215.7 11.9 fusion.23
  227.6 10.7 all-to-all-start.1
  238.3 320.4 %all_gather.42 = bf16[1024,64]{1,0:T(8,128)(2,1)S(1)} all-gather(bf16[8,64]{1,0:T(8,128)(2,1)S(1)} %copy-done.40), channel_id=1, replica_groups=mesh['dp'=2,'expert'=64] {'dp','expert'}, dimensions={0}, use_global_device_ids=true | all-gather | bytes 132096 | tf_op jit(solution)/shard_map/all_gather | solution.py:78
  564.1 23.3 %all_to_all.20 = bf16[64,8,1024]{2,1,0:T(8,128)(2,1)S(1)} all-to-all(bf16[64,8,1024]{2,1,0:T(8,128)(2,1)S(1)} %fusion.30), channel_id=1, replica_groups=mesh['dp'=2,'expert'=64] {'expert'}, dimensions={0} | all-to-all | bytes 2097152 | tf_op jit(solution)/shard_map/all_to_all | solution.py:175
  587.4 12.8 fusion.6
  602.3 5.6 fusion.26
  607.9 4.7 all-to-all-start.3
  617.3 13.0 all-to-all-done.3
  635.2 3.2 convolution_convert_fusion.1
  638.5 6.1 multiply_reduce_fusion
  652.9 10.5 convert_bitcast_fusion.1
  664.6 12.6 convert_bitcast_fusion
  678.2 2.7 fusion.69
  681.0 3.6 fusion.32
  684.6 7.9 fusion.62
  693.1 118.3 %all-reduce.13.cloned.1.call-done = f32[1024,64]{1,0:T(8,128)} async-done(((f32[1024,64]{1,0:T(8,128)}), f32[1024,64]{1,0:T(8,128)}) %all-reduce.13.cloned.1.call-update) | async-done | bytes 262160
  812.7 5.2 fusion.46
  818.0 66.0 %all-reduce.9 = (f32[]{:T(128)}, f32[]{:T(128)}, f32[1024]{0:T(1024)S(1)}, f32[1024]{0:T(1024)S(1)}, f32[1024]{0:T(1024)S(1)}, /*index=5*/f32[1024]{0:T(1024)S(1)}) all-reduce(f32[]{:T(128)} %get-tuple-element.19, f32[]{:T(128)} %fusion.89, f32[1024]{0:T(1024)S(1)} %get-tuple-element.14, ...), channel_id=1, replica_groups=mesh['dp'=2,'expert'=64] {'dp','expert'}, use_global_device_ids=true, to_apply=%region_13.14 | all-reduce | flops 4098 | bytes 32784 | tf_op jit(solution)/shard_map/psum | solution.py:152
  888.9 6.7 convert_element_type.163
  895.6 6.6 convert_element_type.166
  902.3 617.3 %reduce-scatter.10.cloned.1.call-done = f32[8,1024]{1,0:T(8,128)} async-done(((f32[1024,1024]{1,0:T(8,128)}), f32[8,1024]{1,0:T(8,128)}) %reduce-scatter.10.cloned.1.call-update) | async-done | bytes 32784 | tf_op jit(solution)/shard_map/reduce_scatter | solution.py:232
  1519.6 223.2 %reduce-scatter.8.cloned.1.call-done = f32[8,3072]{1,0:T(8,128)} async-done(((f32[1024,3072]{1,0:T(8,128)}), f32[8,3072]{1,0:T(8,128)}) %reduce-scatter.8.cloned.1.call-update) | async-done | bytes 98320 | tf_op jit(solution)/shard_map/reduce_scatter | solution.py:231
  (189 shorter events, 61.4 us)
Async XLA Ops:
  7.2 75.9 %all-gather.6.cloned.1.call-start = ((), (), s32[]{:S(2)}) async-start(), calls=%async_computation.9 | async-start | bytes 6340608 | tf_op jit(solution)/shard_map/all_gather | solution.py:74
  7.9 91.3 %all-gather.8.cloned.1.call-start = ((), (), s32[]{:S(2)}) async-start(), calls=%async_computation.10 | async-start | bytes 3145728 | tf_op jit(solution)/shard_map/all_gather | solution.py:97
  80.4 7.5 copy-start.23
  80.5 7.5 copy-start.21
  89.1 79.7 %all-gather.10.cloned.1.call-start = ((), (), s32[]{:S(2)}) async-start(), calls=%async_computation.11 | async-start | bytes 2113536 | tf_op jit(solution)/shard_map/all_gather | solution.py:75
  89.8 100.5 %all-gather.12.cloned.1.call-start = ((), (), s32[]{:S(2)}) async-start(), calls=%async_computation.12 | async-start | bytes 12582912 | tf_op jit(solution)/shard_map/all_gather | solution.py:81
  90.4 125.3 %all-gather.14.cloned.1.call-start = ((), (), s32[]{:S(2)}) async-start(), calls=%async_computation.13 | async-start | bytes 12582912 | tf_op jit(solution)/shard_map/all_gather | solution.py:82
  91.6 79.9 %copy-start.25 = (f32[1024]{0:T(1024)}, f32[1024]{0:T(1024)S(1)}, u32[]{:S(2)}) copy-start(f32[1024]{0:T(1024)S(1)} %convert_element_type.138) | copy-start | bytes 12292
  92.7 79.1 %copy-start.37 = (s32[256]{0:T(256)}, s32[256]{0:T(256)S(1)}, u32[]{:S(2)}) copy-start(s32[256]{0:T(256)S(1)} %multiply_add_fusion.1) | copy-start | bytes 3076
  93.1 13.0 copy-start.8
  108.3 60.5 %copy-start.3 = (bf16[1,256,1024]{2,1,0:T(8,128)(2,1)S(1)}, bf16[1,256,1024]{2,1,0:T(8,128)(2,1)}, u32[]{:S(2)}) copy-start(bf16[1,256,1024]{2,1,0:T(8,128)(2,1)} %param.13) | copy-start | bytes 1572868
  113.9 57.6 %copy-start.10 = (bf16[16,64,256]{2,1,0:T(8,128)(2,1)}, bf16[16,64,256]{2,1,0:T(8,128)(2,1)S(1)}, u32[]{:S(2)}) copy-start(bf16[16,64,256]{2,1,0:T(8,128)(2,1)S(1)} %convolution_convert_fusion.4) | copy-start | bytes 1572868
  171.2 39.4 %copy-start.31 = (f32[256]{0:T(256)}, f32[256]{0:T(256)S(1)}, u32[]{:S(2)}) copy-start(f32[256]{0:T(256)S(1)} %broadcast_multiply_fusion.4) | copy-start | bytes 3076
  171.5 39.1 %copy-start.36 = (f32[256]{0:T(256)}, f32[256]{0:T(256)S(1)}, u32[]{:S(2)}) copy-start(f32[256]{0:T(256)S(1)} %add_rsqrt_fusion) | copy-start | bytes 3076
  173.2 25.5 %all-to-all-start = ((bf16[64,8,1024]{2,1,0:T(8,128)(2,1)}), bf16[64,8,1024]{2,1,0:T(8,128)(2,1)S(1)}, u32[]{:S(2)}, u32[]{:S(2)}) async-start(bf16[64,8,1024]{2,1,0:T(8,128)(2,1)} %fusion.29), calls=%async_computation | async-start | bytes 2097152 | tf_op jit(solution)/shard_map/all_to_all | solution.py:137
  210.6 27.6 %copy-start.40 = (bf16[8,64]{1,0:T(8,128)(2,1)S(1)}, bf16[8,64]{1,0:T(8,128)(2,1)}, u32[]{:S(2)}) copy-start(bf16[8,64]{1,0:T(8,128)(2,1)} %param.23) | copy-start | bytes 3076
  210.6 349.0 %copy-start.27 = (s32[1,256,1]{1,2,0:T(1,128)S(1)}, s32[1,256,1]{1,2,0:T(1,128)}, u32[]{:S(2)}) copy-start(s32[1,256,1]{1,2,0:T(1,128)} %param.16) | copy-start | bytes 3076
  210.6 349.6 %copy-start.12 = (bf16[1,256,1024]{2,1,0:T(8,128)(2,1)S(1)}, bf16[1,256,1024]{2,1,0:T(8,128)(2,1)}, u32[]{:S(2)}) copy-start(bf16[1,256,1024]{2,1,0:T(8,128)(2,1)} %param.14) | copy-start | bytes 1572868
  227.6 332.7 %all-to-all-start.1 = ((bf16[64,8,1024]{2,1,0:T(8,128)(2,1)}), bf16[64,8,1024]{2,1,0:T(8,128)(2,1)}, u32[]{:S(2)}, u32[]{:S(2)}) async-start(bf16[64,8,1024]{2,1,0:T(8,128)(2,1)} %fusion.23), calls=%async_computation.1 | async-start | bytes 2097152 | tf_op jit(solution)/shard_map/all_to_all | solution.py:147
  562.9 37.4 %copy-start.13 = (bf16[256,1024]{1,0:T(8,128)(2,1)}, bf16[256,1024]{1,0:T(8,128)(2,1)S(1)}, u32[]{:S(2)}) copy-start(bf16[256,1024]{1,0:T(8,128)(2,1)S(1)} %get-tuple-element.32) | copy-start | bytes 1572868
  564.1 38.1 %slice-start.2 = ((s8[8388608]{0:T(1024)(128)(4,1)}), s8[4194304]{0:T(1024)(128)(4,1)S(1)}, s32[]{:S(2)}) async-start(s8[8388608]{0:T(1024)(128)(4,1)} %bitcast.189), calls=%async_computation.22 | async-start | bytes 8388608
  587.4 12.9 copy-start.17
  587.4 14.8 slice-start.3
  607.9 22.5 %all-to-all-start.3 = ((bf16[64,8,1024]{2,1,0:T(8,128)(2,1)}), bf16[64,8,1024]{2,1,0:T(8,128)(2,1)S(1)}, u32[]{:S(2)}, u32[]{:S(2)}) async-start(bf16[64,8,1024]{2,1,0:T(8,128)(2,1)} %fusion.26), calls=%async_computation.3 | async-start | bytes 2097152 | tf_op jit(solution)/shard_map/all_to_all | solution.py:187
  612.6 72.0 %reduce-scatter.6.cloned.1.call-start = ((), (), s32[]{:S(2)}) async-start(), calls=%async_computation.14 | async-start | bytes 3145728 | tf_op jit(solution)/shard_map/reduce_scatter | solution.py:220
  635.2 9.3 slice-start
  651.3 160.2 %all-reduce.13.cloned.1.call-start = ((), (), s32[]{:S(2)}) async-start(), calls=%async_computation.19 | async-start | bytes 1048576
  652.9 236.1 %reduce-scatter.12.cloned.1.call-start = ((), (), s32[]{:S(2)}) async-start(), calls=%async_computation.17 | async-start | bytes 12582912 | tf_op jit(solution)/shard_map/reduce_scatter | solution.py:240
  663.4 232.2 %reduce-scatter.14.cloned.1.call-start = ((), (), s32[]{:S(2)}) async-start(), calls=%async_computation.18 | async-start | bytes 12582912 | tf_op jit(solution)/shard_map/reduce_scatter | solution.py:243
  677.2 7.4 copy-start.22
  677.3 842.3 %reduce-scatter.10.cloned.1.call-start = ((), (), s32[]{:S(2)}) async-start(), calls=%async_computation.16 | async-start | bytes 4227072 | tf_op jit(solution)/shard_map/reduce_scatter | solution.py:232
  680.9 1061.9 %reduce-scatter.8.cloned.1.call-start = ((), (), s32[]{:S(2)}) async-start(), calls=%async_computation.15 | async-start | bytes 12681216 | tf_op jit(solution)/shard_map/reduce_scatter | solution.py:231
  (28 other events, 104.1 us)
Sparse Core Ops, SparseCore 0:
  11.1 70.7 all-gather.5
  89.2 9.9 all-gather.7
  102.2 66.5 all-gather.9
  170.3 19.9 all-gather.11
  191.8 23.8 all-gather.13
  651.4 7.8 reduce-scatter.5
  665.4 146.0 all-reduce.12
  814.4 18.7 reduce-scatter.11
  835.8 20.9 reduce-scatter.13
  859.5 659.9 reduce-scatter.9
  1525.9 216.8 reduce-scatter.7
where the time goes:
time: 1760 us; the launch traced here: 1750 us
  waiting for transfers between devices  1060 us (60%)
  blocking collectives  479 us (27%)
  matrix products  117 us (7%)
  other arithmetic  32.5 us (2%)
  starting transfers between devices  22.7 us (1%)
  local copies, waits for them, and re-layouts  22.6 us (1%)
  between operations  18.2 us (1%)
    reduce_scatter x1, waiting for transfers between devices, per_device(): lax.psum_scatter(grad_out, ('dp', 'expert'), scatter_dimension=0, tiled=T...  617 us
    all_gather x1, blocking collectives, per_device(): lax.all_gather(layer_shards[6], ('dp', 'expert'), axis=0, tiled=True)  320 us
    reduce_scatter x1, waiting for transfers between devices, per_device(): lax.psum_scatter(grad_qkv, ('dp', 'expert'), scatter_dimension=0, tiled=T...  223 us
    unnamed x12, waiting for transfers between devices  121 us
    unnamed x1, blocking collectives  69.1 us
    psum x1, blocking collectives, per_device(): lax.psum((jnp.sum(valid_rows[:, None] * errors * errors), jnp.sum(valid_r...  66 us
    all_gather x1, waiting for transfers between devices, per_device(): lax.all_gather(layer_shards[3], ('dp', 'expert'), axis=0, tiled=True)  54.9 us
    dot_general x6, matrix products, transposed_times(): lax.dot_general(left_mat, right_mat, (((0,), (0,)), ((), ())), preferred_...  38.4 us
  transfers between devices with their start and end apart: 14, of which 9 were waited for; matrix products, arithmetic and copies ran while one was open for 6% of the time, Pallas kernels for 0%

commit v1 on v0

--- a/solution.py
+++ b/solution.py
@@ -72,7 +72,15 @@
         lax.all_gather(layer_shards[0], ("dp", "expert"), axis=0, tiled=True),
         lax.all_gather(layer_shards[1], ("dp", "expert"), axis=0, tiled=True),
         lax.all_gather(layer_shards[2], ("dp", "expert"), axis=0, tiled=True),
-        lax.all_gather(layer_shards[3], ("dp", "expert"), axis=0, tiled=True),
+        jnp.concatenate(
+            lax.all_to_all(
+                jnp.stack([layer_shards[3]] * lax.axis_size(("dp", "expert"))),
+                ("dp", "expert"),
+                0,
+                0,
+            ),
+            axis=0,
+        ),
         lax.all_gather(layer_shards[4], ("dp", "expert"), axis=0, tiled=True),
         lax.all_gather(layer_shards[5], ("dp", "expert"), axis=0, tiled=True),
         lax.all_gather(layer_shards[6], ("dp", "expert"), axis=0, tiled=True),

time: 1760 us -> 1710 us (0.972)
  waiting for transfers between devices: 1060 us -> 1030 us
  blocking collectives: 479 us -> 453 us
    all_gather x1, waiting for transfers between devices: 54.9 us -> 3.38 us  [per_device(): lax.all_gather(layer_shards[3], ('dp', 'expert'), axis=0, tiled=True)]
    all_to_all x0 -> x2, waiting for transfers between devices: none -> 29.3 us  [the longest x1 18.9 us: per_device(): lax.all_to_all(d_send.reshape(sources, capacity, width), 'expert', split_...]
    all_to_all x1 -> x0, blocking collectives: 23.3 us -> none  [per_device(): lax.all_to_all(d_send.reshape(sources, capacity, width), 'expert', split_...]
  transfers between devices with their start and end apart: 14 -> 16, of which waited for: 9 -> 8; matrix products, arithmetic and copies ran while one was open for 6% -> 8% of each run, Pallas kernels for 0% -> 0%
where the time goes in v1:
time: 1710 us
  waiting for transfers between devices  1030 us (60%)
  blocking collectives  453 us (26%)
  matrix products  121 us (7%)
  other arithmetic  32.5 us (2%)
  starting transfers between devices  30.6 us (2%)
  local copies, waits for them, and re-layouts  24.2 us (1%)
  between operations  18.1 us (1%)
    reduce_scatter x1, waiting for transfers between devices, per_device(): lax.psum_scatter(grad_out, ('dp', 'expert'), scatter_dimension=0, tiled=T...  617 us
    all_gather x1, blocking collectives, per_device(): lax.all_gather(layer_shards[6], ('dp', 'expert'), axis=0, tiled=True)  318 us
    reduce_scatter x1, waiting for transfers between devices, per_device(): lax.psum_scatter(grad_qkv, ('dp', 'expert'), scatter_dimension=0, tiled=T...  223 us
    unnamed x12, waiting for transfers between devices  123 us
    unnamed x1, blocking collectives  69.1 us
    psum x1, blocking collectives, per_device(): lax.psum((jnp.sum(valid_rows[:, None] * errors * errors), jnp.sum(valid_r...  66 us
    dot_general x6, matrix products, transposed_times(): lax.dot_general(left_mat, right_mat, (((0,), (0,)), ((), ())), preferred_...  38.5 us
  transfers between devices with their start and end apart: 16, of which 8 were waited for; matrix products, arithmetic and copies ran while one was open for 8% of the time, Pallas kernels for 0%

profile of v1, /device:TPU:0, one launch (start us, length us, event | category | flops | bytes accessed | tf_op | source)
XLA Modules:
  0.0 1709.2 jit_solution(17688764414047888734)
XLA Ops:
  11.3 69.1 %all-reduce.10 = (bf16[1024]{0:T(1024)(128)(2,1)S(1)}, bf16[1024]{0:T(1024)(128)(2,1)S(1)}, bf16[1024]{0:T(1024)(128)(2,1)S(1)}, bf16[1024]{0:T(1024)(128)(2,1)S(1)}) all-reduce(bf16[1024]{0:T(1024)(128)(2,1)S(1)} %dynamic-update-slice.1, bf16[1024]{0:T(1024)(128)(2,1)S(1)} %dynamic-update-slice, ...), channel_id=1, replica_groups=mesh['dp'=2,'expert'=64] {'dp','expert'}, use_global_device_ids=true, to_apply=%add.1 | all-reduce | flops 4096 | bytes 16384
  83.6 4.9 convolution_convert_fusion
  92.5 6.0 all-to-all-start
  100.6 2.9 fusion.99
  115.8 10.4 all-to-all-done
  130.6 7.7 all-to-all-start.1
  138.3 18.8 %all-to-all-done.1 = bf16[64,8,1024]{2,1,0:T(8,128)(2,1)S(1)} async-done(((bf16[64,8,1024]{2,1,0:T(8,128)(2,1)}), bf16[64,8,1024]{2,1,0:T(8,128)(2,1)S(1)}, u32[]{:S(2)}, u32[]{:S(2)}) %all-to-all-start.1) | async-done | bytes 1048608 | tf_op jit(solution)/shard_map/all_to_all | solution.py:145
  158.1 10.1 fusion.13
  168.2 11.9 fusion.25
  180.1 5.5 all-to-all-start.2
  185.7 318.4 %all_gather.40 = bf16[1024,64]{1,0:T(8,128)(2,1)S(1)} all-gather(bf16[8,64]{1,0:T(8,128)(2,1)S(1)} %copy-done.38), channel_id=1, replica_groups=mesh['dp'=2,'expert'=64] {'dp','expert'}, dimensions={0}, use_global_device_ids=true | all-gather | bytes 132096 | tf_op jit(solution)/shard_map/all_gather | solution.py:86
  510.5 5.6 all-to-all-start.3
  516.7 18.9 %all-to-all-done.3 = bf16[64,8,1024]{2,1,0:T(8,128)(2,1)} async-done(((bf16[64,8,1024]{2,1,0:T(8,128)(2,1)}), bf16[64,8,1024]{2,1,0:T(8,128)(2,1)}, u32[]{:S(2)}, u32[]{:S(2)}) %all-to-all-start.3) | async-done | bytes 1048608 | tf_op jit(solution)/shard_map/all_to_all | solution.py:183
  535.6 12.7 fusion.6
  550.2 8.2 fusion.28
  558.4 4.7 all-to-all-start.4
  567.8 14.6 all-to-all-done.4
  586.2 3.4 all-gather.14.cloned.1.call-done
  592.1 3.2 convolution_convert_fusion.1
  595.3 6.1 multiply_reduce_fusion
  609.8 10.5 convert_bitcast_fusion.1
  620.6 12.8 convert_bitcast_fusion
  634.4 2.7 fusion.74
  637.2 3.6 fusion.37
  640.8 7.9 fusion.67
  649.3 120.6 %all-reduce.13.cloned.1.call-done = f32[1024,64]{1,0:T(8,128)} async-done(((f32[1024,64]{1,0:T(8,128)}), f32[1024,64]{1,0:T(8,128)}) %all-reduce.13.cloned.1.call-update) | async-done | bytes 262160
  771.2 5.3 fusion.51
  776.4 66.0 %all-reduce.9 = (f32[]{:T(128)}, f32[]{:T(128)}, f32[1024]{0:T(1024)S(1)}, f32[1024]{0:T(1024)S(1)}, f32[1024]{0:T(1024)S(1)}, /*index=5*/f32[1024]{0:T(1024)S(1)}) all-reduce(f32[]{:T(128)} %get-tuple-element.19, f32[]{:T(128)} %fusion.94, f32[1024]{0:T(1024)S(1)} %get-tuple-element.14, ...), channel_id=1, replica_groups=mesh['dp'=2,'expert'=64] {'dp','expert'}, use_global_device_ids=true, to_apply=%region_13.14 | all-reduce | flops 4098 | bytes 32784 | tf_op jit(solution)/shard_map/psum | solution.py:160
  847.4 6.7 convert_element_type.165
  854.1 6.6 convert_element_type.168
  860.8 617.3 %reduce-scatter.10.cloned.1.call-done = f32[8,1024]{1,0:T(8,128)} async-done(((f32[1024,1024]{1,0:T(8,128)}), f32[8,1024]{1,0:T(8,128)}) %reduce-scatter.10.cloned.1.call-update) | async-done | bytes 32784 | tf_op jit(solution)/shard_map/reduce_scatter | solution.py:240
  1478.1 223.2 %reduce-scatter.8.cloned.1.call-done = f32[8,3072]{1,0:T(8,128)} async-done(((f32[1024,3072]{1,0:T(8,128)}), f32[8,3072]{1,0:T(8,128)}) %reduce-scatter.8.cloned.1.call-update) | async-done | bytes 98320 | tf_op jit(solution)/shard_map/reduce_scatter | solution.py:239
  (184 shorter events, 65.3 us)
Async XLA Ops:
  7.2 75.9 %all-gather.6.cloned.1.call-start = ((), (), s32[]{:S(2)}) async-start(), calls=%async_computation.10 | async-start | bytes 6340608 | tf_op jit(solution)/shard_map/all_gather | solution.py:74
  7.9 92.7 %all-gather.8.cloned.1.call-start = ((), (), s32[]{:S(2)}) async-start(), calls=%async_computation.11 | async-start | bytes 3145728 | tf_op jit(solution)/shard_map/all_gather | solution.py:105
  80.4 8.0 copy-start.20
  80.5 8.0 copy-start.18
  89.6 9.6 copy-start.24
  89.6 48.7 %all-gather.10.cloned.1.call-start = ((), (), s32[]{:S(2)}) async-start(), calls=%async_computation.12 | async-start | bytes 12582912 | tf_op jit(solution)/shard_map/all_gather | solution.py:89
  90.3 77.9 %all-gather.12.cloned.1.call-start = ((), (), s32[]{:S(2)}) async-start(), calls=%async_computation.13 | async-start | bytes 12582912 | tf_op jit(solution)/shard_map/all_gather | solution.py:90
  92.5 33.6 %all-to-all-start = ((bf16[128,8,1024]{2,1,0:T(8,128)(2,1)}), bf16[128,8,1024]{2,1,0:T(8,128)(2,1)}, u32[]{:S(2)}, u32[]{:S(2)}) async-start(bf16[128,8,1024]{2,1,0:T(8,128)(2,1)} %stack.2), calls=%async_computation | async-start | bytes 4194304 | tf_op jit(solution)/shard_map/all_to_all | solution.py:76
  99.1 29.7 %copy-start.22 = (f32[1024]{0:T(1024)}, f32[1024]{0:T(1024)S(1)}, u32[]{:S(2)}) copy-start(f32[1024]{0:T(1024)S(1)} %convert_element_type.140) | copy-start | bytes 12292
  100.1 29.0 %copy-start.35 = (s32[256]{0:T(256)}, s32[256]{0:T(256)S(1)}, u32[]{:S(2)}) copy-start(s32[256]{0:T(256)S(1)} %multiply_add_fusion.1) | copy-start | bytes 3076
  109.9 16.2 copy-start.3
  115.8 13.1 copy-start.9
  128.6 39.6 %copy-start.29 = (f32[256]{0:T(256)}, f32[256]{0:T(256)S(1)}, u32[]{:S(2)}) copy-start(f32[256]{0:T(256)S(1)} %broadcast_multiply_fusion.4) | copy-start | bytes 3076
  128.9 39.3 %copy-start.34 = (f32[256]{0:T(256)}, f32[256]{0:T(256)S(1)}, u32[]{:S(2)}) copy-start(f32[256]{0:T(256)S(1)} %add_rsqrt_fusion) | copy-start | bytes 3076
  130.6 26.5 %all-to-all-start.1 = ((bf16[64,8,1024]{2,1,0:T(8,128)(2,1)}), bf16[64,8,1024]{2,1,0:T(8,128)(2,1)S(1)}, u32[]{:S(2)}, u32[]{:S(2)}) async-start(bf16[64,8,1024]{2,1,0:T(8,128)(2,1)} %fusion.31), calls=%async_computation.1 | async-start | bytes 2097152 | tf_op jit(solution)/shard_map/all_to_all | solution.py:145
  168.2 17.5 %copy-start.38 = (bf16[8,64]{1,0:T(8,128)(2,1)S(1)}, bf16[8,64]{1,0:T(8,128)(2,1)}, u32[]{:S(2)}) copy-start(bf16[8,64]{1,0:T(8,128)(2,1)} %param.23) | copy-start | bytes 3076
  168.2 336.8 %copy-start.25 = (s32[1,256,1]{1,2,0:T(1,128)S(1)}, s32[1,256,1]{1,2,0:T(1,128)}, u32[]{:S(2)}) copy-start(s32[1,256,1]{1,2,0:T(1,128)} %param.16) | copy-start | bytes 3076
  168.2 337.5 %copy-start.11 = (bf16[1,256,1024]{2,1,0:T(8,128)(2,1)S(1)}, bf16[1,256,1024]{2,1,0:T(8,128)(2,1)}, u32[]{:S(2)}) copy-start(bf16[1,256,1024]{2,1,0:T(8,128)(2,1)} %param.14) | copy-start | bytes 1572868
  180.1 325.5 %all-to-all-start.2 = ((bf16[64,8,1024]{2,1,0:T(8,128)(2,1)}), bf16[64,8,1024]{2,1,0:T(8,128)(2,1)}, u32[]{:S(2)}, u32[]{:S(2)}) async-start(bf16[64,8,1024]{2,1,0:T(8,128)(2,1)} %fusion.25), calls=%async_computation.2 | async-start | bytes 2097152 | tf_op jit(solution)/shard_map/all_to_all | solution.py:155
  508.2 40.0 %copy-start.12 = (bf16[256,1024]{1,0:T(8,128)(2,1)}, bf16[256,1024]{1,0:T(8,128)(2,1)S(1)}, u32[]{:S(2)}) copy-start(bf16[256,1024]{1,0:T(8,128)(2,1)S(1)} %get-tuple-element.32) | copy-start | bytes 1572868
  510.5 25.1 %all-to-all-start.3 = ((bf16[64,8,1024]{2,1,0:T(8,128)(2,1)}), bf16[64,8,1024]{2,1,0:T(8,128)(2,1)}, u32[]{:S(2)}, u32[]{:S(2)}) async-start(bf16[64,8,1024]{2,1,0:T(8,128)(2,1)} %fusion.32), calls=%async_computation.3 | async-start | bytes 2097152 | tf_op jit(solution)/shard_map/all_to_all | solution.py:183
  516.1 73.5 %all-gather.14.cloned.1.call-start = ((), (), s32[]{:S(2)}) async-start(), calls=%async_computation.14 | async-start | bytes 2113536 | tf_op jit(solution)/shard_map/all_gather | solution.py:168
  558.4 24.0 %all-to-all-start.4 = ((bf16[64,8,1024]{2,1,0:T(8,128)(2,1)}), bf16[64,8,1024]{2,1,0:T(8,128)(2,1)S(1)}, u32[]{:S(2)}, u32[]{:S(2)}) async-start(bf16[64,8,1024]{2,1,0:T(8,128)(2,1)} %fusion.28), calls=%async_computation.4 | async-start | bytes 2097152 | tf_op jit(solution)/shard_map/all_to_all | solution.py:195
  563.0 77.7 %reduce-scatter.6.cloned.1.call-start = ((), (), s32[]{:S(2)}) async-start(), calls=%async_computation.15 | async-start | bytes 3145728 | tf_op jit(solution)/shard_map/reduce_scatter | solution.py:228
  584.5 10.8 copy-start.17
  592.1 9.3 slice-start
  608.1 161.8 %all-reduce.13.cloned.1.call-start = ((), (), s32[]{:S(2)}) async-start(), calls=%async_computation.20 | async-start | bytes 1048576
  609.8 237.7 %reduce-scatter.12.cloned.1.call-start = ((), (), s32[]{:S(2)}) async-start(), calls=%async_computation.18 | async-start | bytes 12582912 | tf_op jit(solution)/shard_map/reduce_scatter | solution.py:248
  620.3 233.8 %reduce-scatter.14.cloned.1.call-start = ((), (), s32[]{:S(2)}) async-start(), calls=%async_computation.19 | async-start | bytes 12582912 | tf_op jit(solution)/shard_map/reduce_scatter | solution.py:251
  633.4 7.4 copy-start.19
  633.4 844.6 %reduce-scatter.10.cloned.1.call-start = ((), (), s32[]{:S(2)}) async-start(), calls=%async_computation.17 | async-start | bytes 4227072 | tf_op jit(solution)/shard_map/reduce_scatter | solution.py:240
  637.1 1064.2 %reduce-scatter.8.cloned.1.call-start = ((), (), s32[]{:S(2)}) async-start(), calls=%async_computation.16 | async-start | bytes 12681216 | tf_op jit(solution)/shard_map/reduce_scatter | solution.py:239
  (26 other events, 90.3 us)
Sparse Core Ops, SparseCore 0:
  11.1 70.7 all-gather.5
  89.7 9.4 all-gather.7
  100.9 23.8 all-gather.9
  126.3 23.8 all-gather.11
  519.6 69.9 all-gather.13
  608.3 9.4 reduce-scatter.5
  623.9 146.0 all-reduce.12
  772.9 18.7 reduce-scatter.11
  794.3 20.9 reduce-scatter.13
  818.0 659.9 reduce-scatter.9
  1484.4 216.8 reduce-scatter.7
